TPU v7x, 512 devices: a whole 4x8x8 slice. The times are simulated.
512 devices in a mesh: dp: 64 (over y, z), factor: 8 (over x, core).
Axes of the slice: x: 4, y: 8, z: 8, core: 2. Of those that a mesh axis runs over, the one named last changes fastest.
Arguments:
- layer_inputs: bfloat16 [65536, 5120], P('dp', 'factor'), may hold values from -64 to 64
- out_grads: bfloat16 [65536, 5120], P('dp', 'factor'), may hold values from -64 to 64
- weight_grad: bfloat16 [5120, 5120], P('dp', 'factor'), may hold values from -32 to 32
- left_inv: float32 [5120, 5120], P('dp', 'factor'), may hold values from -4 to 10, as said below
- right_inv: float32 [5120, 5120], P('factor', 'dp'), may hold values from -4 to 10, as said below
Outputs:
- precond_grad: bfloat16 [5120, 5120], P('dp', 'factor')
- new_left: float32 [5120, 5120], P('dp', 'factor')
- new_right: float32 [5120, 5120], P('factor', 'dp')
Inputs may be any that keep to these rules, and one draw needn't show every extreme that they name: `left_inv`: symmetric and positive definite, every eigenvalue 0.1 or more. `right_inv`: symmetric and positive definite, every eigenvalue 0.1 or more.
All inputs are finite; a program needn't handle non-finite values.
Results may differ from a plain program's by a relative error of at most 0.00275.
The roundings to bfloat16 on the way count: a program that leaves them out, or rounds other values in their place, can miss the bound.
Values may be sent and summed in bfloat16 or wider, within the bound.
No kernel may reach another device: no remote copies, remote signals or barrier semaphores. Data moves between devices by JAX's collectives and lax.ppermute only.
A program may use at most 64 MiB of HBM per device.

v0:
```python
import jax
import jax.numpy as jnp
from jax import lax
from jax.sharding import Mesh, PartitionSpec as P

decay = 0.9
PAD = 104


def coefficient(quadratic):
    return (1.0 - decay) / (decay * decay * (1.0 + (1.0 - decay) / decay * quadratic))


def share(vec, axes, count):
    return lax.all_to_all(jnp.broadcast_to(vec[None], (count,) + vec.shape), axes, 0, 0, tiled=True)


def gather_rows(block, axis, count):
    rows, cols = block.shape
    padded = jnp.pad(block, ((0, PAD - rows), (0, 0)))
    whole = lax.all_gather(padded, axis, axis=0, tiled=False)
    return whole[:, :rows, :].reshape(count * rows, cols)


def per_device(layer_inputs, out_grads, weight_grad, left_inv, right_inv):
    ny, nz, nf = (lax.axis_size("y"), lax.axis_size("z"), lax.axis_size("f"))
    token_count = layer_inputs.shape[0] * ny * nz
    rows, cols = left_inv.shape
    y, z, f = (lax.axis_index("y"), lax.axis_index("z"), lax.axis_index("f"))
    left_wide = lax.all_gather(left_inv, "y", axis=0, tiled=True)
    swap = [(a * nf + b, b * nf + a) for a in range(ny) for b in range(nf)]
    weight_piece = lax.ppermute(weight_grad, ("y", "f"), swap)
    act_local = jnp.sum(layer_inputs, axis=0, dtype=jnp.float32)
    grad_local = jnp.sum(out_grads, axis=0, dtype=jnp.float32)
    sums = share(jnp.concatenate([act_local, grad_local]), ("y", "z"), ny * nz)
    means = jnp.sum(sums, axis=0) / token_count
    mean_act, mean_grad = (means[:cols], means[cols:])
    weight_piece, means = lax.optimization_barrier((weight_piece, means))
    weight_block = gather_rows(weight_piece, "z", nz)
    left_partial = jnp.sum(left_inv * means[None, :cols], axis=1)
    right_partial = jnp.sum(right_inv * means[cols:, None], axis=0)
    both = share(jnp.concatenate([means, left_partial, right_partial]), "f", nf)
    whole_act = both[:, :cols].reshape(nf * cols)
    whole_grad = both[:, cols : 2 * cols].reshape(nf * cols)
    images = jnp.sum(both[:, 2 * cols :], axis=0)
    all_images = share(images, ("y", "z"), ny * nz)
    left_image = all_images[:, :rows].reshape(ny * nz * rows)
    right_image = all_images[:, rows:].reshape(ny * nz * rows)
    left_coef = coefficient(jnp.sum(whole_act * left_image))
    right_coef = coefficient(jnp.sum(whole_grad * right_image))
    left_cols = lax.dynamic_slice_in_dim(left_image, f * cols, cols)
    right_rows = lax.dynamic_slice_in_dim(right_image, f * cols, cols)
    new_left = left_inv / decay - left_coef * images[:rows, None] * left_cols[None, :]
    new_right = right_inv / decay - right_coef * right_rows[:, None] * images[None, rows:]
    right_block = gather_rows(new_right.astype(jnp.bfloat16).T, "z", nz)
    wide_rows = lax.dynamic_slice_in_dim(left_image.reshape(ny, nz, rows), z, 1, 1).reshape(
        ny * rows
    )
    left_block = left_wide / decay - left_coef * wide_rows[:, None] * left_cols[None, :]
    partial = jnp.dot(
        left_block.astype(jnp.bfloat16), weight_block, preferred_element_type=jnp.float32
    )
    pieces = lax.all_to_all(partial.reshape(nf, ny * rows // nf, cols), "f", 0, 0, tiled=True)
    hidden_piece = jnp.sum(pieces, axis=0).astype(jnp.bfloat16)
    hidden = lax.all_gather(hidden_piece, "f", axis=0, tiled=True)
    partial = jnp.dot(hidden, right_block, preferred_element_type=jnp.float32)
    pieces = lax.all_to_all(partial.reshape(ny, rows, cols), "y", 0, 0, tiled=True)
    precond = jnp.sum(pieces, axis=0).astype(jnp.bfloat16)
    return (precond, new_left, new_right)


def solution(mesh):
    cube = Mesh(mesh.devices.reshape(8, 8, 8), ("y", "z", "f"))
    rows, cols = (P(("y", "z"), "f"), P("f", ("y", "z")))
    return jax.shard_map(
        per_device,
        mesh=cube,
        in_specs=(rows, rows, rows, rows, cols),
        out_specs=(rows, rows, cols),
        check_vma=False,
    )
```

profile of v0, /device:TPU:1, one launch (start us, length us, event | category | flops | bytes accessed | tf_op | source)
XLA Modules:
  0.0 244.4 jit_solution(15196800060828398383)
XLA Ops:
  7.2 2.2 convert_reduce_fusion
  9.4 0.9 broadcast_in_dim.6
  10.3 17.1 %all-to-all-start = ((f32[64,1,1280]{2,1,0:T(1,128)}), f32[64,1,1280]{2,1,0:T(1,128)S(1)}, u32[]{:S(2)}, u32[]{:S(2)}) async-start(f32[64,1,1280]{2,1,0:T(1,128)} %broadcast_in_dim.6), calls=%async_computation | async-start | bytes 655360 | tf_op jit(solution)/shard_map/all_to_all | solution.py:15
  27.4 4.0 %collective-permute-start = (bf16[80,640]{1,0:T(8,128)(2,1)S(1)}, bf16[80,640]{1,0:T(8,128)(2,1)S(1)}, u32[]{:S(2)}, u32[]{:S(2)}) collective-permute-start(bf16[80,640]{1,0:T(8,128)(2,1)S(1)} %copy-done.2), channel_id=1, source_target_pairs={{0,0},{1,64},{2,128},{3,192},{4,256},{5,320},{6,384},{7,448},{64,1... | collective-permute-start | bytes 307208 | tf_op jit(solution)/shard_map/ppermute | solution.py:32
  31.5 9.7 %all-to-all-done = f32[64,1,1280]{2,1,0:T(1,128)S(1)} async-done(((f32[64,1,1280]{2,1,0:T(1,128)}), f32[64,1,1280]{2,1,0:T(1,128)S(1)}, u32[]{:S(2)}, u32[]{:S(2)}) %all-to-all-start) | async-done | bytes 327712 | tf_op jit(solution)/shard_map/all_to_all | solution.py:15
  41.2 0.2 reduce_sum.92
  41.5 0.7 pad.7
  42.2 0.7 all-gather.6.cloned.1.call-update
  42.9 0.1 multiply_reduce_fusion.1
  43.1 0.1 multiply_reduce_fusion
  43.3 16.8 %all_to_all.34 = f32[8,1,1440]{2,1,0:T(1,128)S(1)} all-to-all(f32[8,1,1440]{2,1,0:T(1,128)S(1)} %broadcast_in_dim.7), channel_id=1, replica_groups=mesh['y'=8,'z'=8,'f'=8] {'f'}, dimensions={0} | all-to-all | bytes 92160 | tf_op jit(solution)/shard_map/all_to_all | solution.py:15
  60.1 0.7 broadcast_in_dim.8
  60.8 5.6 %all-to-all-start.2 = ((f32[64,1,160]{2,1,0:T(1,128)}), f32[64,1,160]{2,1,0:T(1,128)S(1)}, u32[]{:S(2)}, u32[]{:S(2)}) async-start(f32[64,1,160]{2,1,0:T(1,128)} %broadcast_in_dim.8), calls=%async_computation.2 | async-start | bytes 131072 | tf_op jit(solution)/shard_map/all_to_all | solution.py:15
  66.5 11.1 %all-to-all-done.2 = f32[64,1,160]{2,1,0:T(1,128)S(1)} async-done(((f32[64,1,160]{2,1,0:T(1,128)}), f32[64,1,160]{2,1,0:T(1,128)S(1)}, u32[]{:S(2)}, u32[]{:S(2)}) %all-to-all-start.2) | async-done | bytes 40992 | tf_op jit(solution)/shard_map/all_to_all | solution.py:15
  77.6 0.1 reshape.66
  78.0 0.6 fusion
  80.1 0.1 dynamic_slice.10
  80.3 0.8 convert_bitcast_fusion
  81.1 0.7 pad.8
  81.8 1.2 slice.47
  83.0 41.1 %all-gather.6.cloned.1.call-done = f32[640,640]{1,0:T(8,128)} async-done(((f32[80,640]{1,0:T(8,128)}), f32[640,640]{1,0:T(8,128)}) %all-gather.6.cloned.1.call-update) | async-done | bytes 1638416 | tf_op jit(solution)/shard_map/all_gather | solution.py:30
  124.1 1.7 subtract_convert_fusion
  125.8 2.1 fusion.4
  127.8 9.1 %all-to-all-start.3 = ((f32[8,80,640]{2,1,0:T(8,128)}), f32[8,80,640]{2,1,0:T(8,128)S(1)}, u32[]{:S(2)}, u32[]{:S(2)}) async-start(f32[8,80,640]{2,1,0:T(8,128)} %fusion.4), calls=%async_computation.3 | async-start | bytes 3276800 | tf_op jit(solution)/shard_map/all_to_all | solution.py:63
  137.0 29.8 %all-gather.10.cloned.1.call-done = bf16[832,640]{1,0:T(8,128)(2,1)} async-done(((bf16[104,640]{1,0:T(8,128)(2,1)}), bf16[832,640]{1,0:T(8,128)(2,1)}) %all-gather.10.cloned.1.call-update) | async-done | bytes 1064976 | tf_op jit(solution)/shard_map/all_gather | solution.py:21
  166.8 1.2 slice.50
  168.1 18.7 %all_gather.21 = bf16[640,640]{1,0:T(8,128)(2,1)S(1)} all-gather(bf16[80,640]{1,0:T(8,128)(2,1)S(1)} %reduce_sum.97), channel_id=1, replica_groups=mesh['y'=8,'z'=8,'f'=8] {'f'}, dimensions={0}, use_global_device_ids=true | all-gather | bytes 921600 | tf_op jit(solution)/shard_map/all_gather | solution.py:65
  186.8 2.1 fusion.5
  188.9 6.5 %all-to-all-start.4 = ((f32[8,80,640]{2,1,0:T(8,128)}), f32[8,80,640]{2,1,0:T(8,128)S(1)}, u32[]{:S(2)}, u32[]{:S(2)}) async-start(f32[8,80,640]{2,1,0:T(8,128)} %fusion.5), calls=%async_computation.4 | async-start | bytes 3276800 | tf_op jit(solution)/shard_map/all_to_all | solution.py:67
  195.3 0.8 multiply_subtract_fusion
  196.1 41.1 %all-to-all-done.4 = f32[8,80,640]{2,1,0:T(8,128)S(1)} async-done(((f32[8,80,640]{2,1,0:T(8,128)}), f32[8,80,640]{2,1,0:T(8,128)S(1)}, u32[]{:S(2)}, u32[]{:S(2)}) %all-to-all-start.4) | async-done | bytes 1638432 | tf_op jit(solution)/shard_map/all_to_all | solution.py:67
  237.2 0.7 reduce_sum.99
  (31 shorter events, 1.0 us)
Async XLA Ops:
  7.2 20.3 %copy-start.2 = (bf16[80,640]{1,0:T(8,128)(2,1)S(1)}, bf16[80,640]{1,0:T(8,128)(2,1)}, u32[]{:S(2)}) copy-start(bf16[80,640]{1,0:T(8,128)(2,1)} %param.7) | copy-start | bytes 307204
  7.2 35.8 %copy-start = (f32[80,640]{1,0:T(8,128)S(1)}, f32[80,640]{1,0:T(8,128)}, u32[]{:S(2)}) copy-start(f32[80,640]{1,0:T(8,128)} %param.8) | copy-start | bytes 614404
  9.4 33.7 %copy-start.1 = (f32[640,80]{0,1:T(8,128)S(1)}, f32[640,80]{0,1:T(8,128)}, u32[]{:S(2)}) copy-start(f32[640,80]{0,1:T(8,128)} %param.9) | copy-start | bytes 614404
  10.3 31.0 %all-to-all-start = ((f32[64,1,1280]{2,1,0:T(1,128)}), f32[64,1,1280]{2,1,0:T(1,128)S(1)}, u32[]{:S(2)}, u32[]{:S(2)}) async-start(f32[64,1,1280]{2,1,0:T(1,128)} %broadcast_in_dim.6), calls=%async_computation | async-start | bytes 655360 | tf_op jit(solution)/shard_map/all_to_all | solution.py:15
  27.4 54.4 %all-gather.8.cloned.1.call-start = ((), (), s32[]{:S(2)}) async-start(), calls=%async_computation.6 | async-start | bytes 1198080 | tf_op jit(solution)/shard_map/all_gather | solution.py:21
  27.4 14.0 %collective-permute-start = (bf16[80,640]{1,0:T(8,128)(2,1)S(1)}, bf16[80,640]{1,0:T(8,128)(2,1)S(1)}, u32[]{:S(2)}, u32[]{:S(2)}) collective-permute-start(bf16[80,640]{1,0:T(8,128)(2,1)S(1)} %copy-done.2), channel_id=1, source_target_pairs={{0,0},{1,64},{2,128},{3,192},{4,256},{5,320},{6,384},{7,448},{64,1... | collective-permute-start | bytes 307208 | tf_op jit(solution)/shard_map/ppermute | solution.py:32
  42.2 81.9 %all-gather.6.cloned.1.call-start = ((), (), s32[]{:S(2)}) async-start(), calls=%async_computation.5 | async-start | bytes 1843200 | tf_op jit(solution)/shard_map/all_gather | solution.py:30
  60.8 16.8 %all-to-all-start.2 = ((f32[64,1,160]{2,1,0:T(1,128)}), f32[64,1,160]{2,1,0:T(1,128)S(1)}, u32[]{:S(2)}, u32[]{:S(2)}) async-start(f32[64,1,160]{2,1,0:T(1,128)} %broadcast_in_dim.8), calls=%async_computation.2 | async-start | bytes 131072 | tf_op jit(solution)/shard_map/all_to_all | solution.py:15
  66.4 100.3 %all-gather.10.cloned.1.call-start = ((), (), s32[]{:S(2)}) async-start(), calls=%async_computation.7 | async-start | bytes 1198080 | tf_op jit(solution)/shard_map/all_gather | solution.py:21
  127.8 40.1 %all-to-all-start.3 = ((f32[8,80,640]{2,1,0:T(8,128)}), f32[8,80,640]{2,1,0:T(8,128)S(1)}, u32[]{:S(2)}, u32[]{:S(2)}) async-start(f32[8,80,640]{2,1,0:T(8,128)} %fusion.4), calls=%async_computation.3 | async-start | bytes 3276800 | tf_op jit(solution)/shard_map/all_to_all | solution.py:63
  188.9 48.3 %all-to-all-start.4 = ((f32[8,80,640]{2,1,0:T(8,128)}), f32[8,80,640]{2,1,0:T(8,128)S(1)}, u32[]{:S(2)}, u32[]{:S(2)}) async-start(f32[8,80,640]{2,1,0:T(8,128)} %fusion.5), calls=%async_computation.4 | async-start | bytes 3276800 | tf_op jit(solution)/shard_map/all_to_all | solution.py:67
Sparse Core Ops, SparseCore 0:
  42.3 38.8 all-gather.7
  83.2 40.7 all-gather.5
  126.2 40.5 all-gather.9
where the time goes:
time: 245 us; the launch traced here: 244 us
  waiting for transfers between devices  134 us (55%)
  starting transfers between devices  42.5 us (17%)
  blocking collectives  35.5 us (14%)
  between operations  15.3 us (6%)
  other arithmetic  7.46 us (3%)
  local copies, waits for them, and re-layouts  6 us (2%)
  matrix products  4.14 us (2%)
    all_to_all x1, waiting for transfers between devices, per_device(): lax.all_to_all(partial.reshape(ny, rows, cols), 'y', 0, 0, tiled=True)  41.1 us
    all_gather x1, waiting for transfers between devices, per_device(): left_wide = lax.all_gather(left_inv, 'y', axis=0, tiled=True)  41.1 us
    all_gather x2, waiting for transfers between devices, gather_rows(): whole = lax.all_gather(padded, axis, axis=0, tiled=False)  29.8 us
    all_to_all x2, starting transfers between devices, share(): lax.all_to_all(jnp.broadcast_to(vec[None], (count,) + vec.shape), axes, 0...  22.8 us
    all_to_all x2, waiting for transfers between devices, share(): lax.all_to_all(jnp.broadcast_to(vec[None], (count,) + vec.shape), axes, 0...  20.8 us
    all_gather x1, blocking collectives, per_device(): hidden = lax.all_gather(hidden_piece, 'f', axis=0, tiled=True)  18.7 us
    all_to_all x1, blocking collectives, share(): lax.all_to_all(jnp.broadcast_to(vec[None], (count,) + vec.shape), axes, 0...  16.8 us
    all_to_all x1, starting transfers between devices, per_device(): lax.all_to_all(partial.reshape(nf, ny * rows // nf, cols), 'f', 0, 0, til...  9.13 us
  transfers between devices with their start and end apart: 8, of which 5 were waited for; matrix products, arithmetic and copies ran while one was open for 4% of the time, Pallas kernels for 0%

commit v1 on v0

--- a/solution.py
+++ b/solution.py
@@ -62,7 +62,10 @@
     )
     pieces = lax.all_to_all(partial.reshape(nf, ny * rows // nf, cols), "f", 0, 0, tiled=True)
     hidden_piece = jnp.sum(pieces, axis=0).astype(jnp.bfloat16)
-    hidden = lax.all_gather(hidden_piece, "f", axis=0, tiled=True)
+    size = lax.axis_size("f")
+    tiles = jnp.stack([hidden_piece for _ in range(size)])
+    tiles = lax.all_to_all(tiles, "f", split_axis=0, concat_axis=0)
+    hidden = jnp.concatenate(tiles, axis=0)
     partial = jnp.dot(hidden, right_block, preferred_element_type=jnp.float32)
     pieces = lax.all_to_all(partial.reshape(ny, rows, cols), "y", 0, 0, tiled=True)
     precond = jnp.sum(pieces, axis=0).astype(jnp.bfloat16)

time: 245 us -> 235 us (0.959); the launches traced: 244 us -> 231 us
  blocking collectives: 35.5 us -> 16.8 us
  starting transfers between devices: 42.5 us -> 47.5 us
    all_to_all x1, waiting for transfers between devices: 0.01 us -> 19.7 us  [per_device(): lax.all_to_all(partial.reshape(nf, ny * rows // nf, cols), 'f', 0, 0, til...]
    all_gather x1 -> x0, blocking collectives: 18.7 us -> none  [per_device(): hidden = lax.all_gather(hidden_piece, 'f', axis=0, tiled=True)]
    all_gather x2, waiting for transfers between devices: 29.8 us -> 13.1 us  [gather_rows(): whole = lax.all_gather(padded, axis, axis=0, tiled=False)]
    all_to_all x0 -> x1, starting transfers between devices: none -> 4.42 us  [per_device(): tiles = lax.all_to_all(tiles, 'f', split_axis=0, concat_axis=0)]
    all_to_all x1, waiting for transfers between devices: 41.1 us -> 37.1 us  [per_device(): lax.all_to_all(partial.reshape(ny, rows, cols), 'y', 0, 0, tiled=True)]
  transfers between devices with their start and end apart: 8 -> 9, of which waited for: 5 -> 7; matrix products, arithmetic and copies ran while one was open for 4% -> 4% of each run, Pallas kernels for 0% -> 0%
where the time goes in v1:
time: 235 us; the launch traced here: 231 us
  waiting for transfers between devices  133 us (57%)
  starting transfers between devices  47.5 us (20%)
  blocking collectives  16.8 us (7%)
  between operations  15.3 us (7%)
  other arithmetic  7.46 us (3%)
  local copies, waits for them, and re-layouts  6.95 us (3%)
  matrix products  4.15 us (2%)
    all_gather x1, waiting for transfers between devices, per_device(): left_wide = lax.all_gather(left_inv, 'y', axis=0, tiled=True)  41.7 us
    all_to_all x1, waiting for transfers between devices, per_device(): lax.all_to_all(partial.reshape(ny, rows, cols), 'y', 0, 0, tiled=True)  37.1 us
    all_to_all x2, starting transfers between devices, share(): lax.all_to_all(jnp.broadcast_to(vec[None], (count,) + vec.shape), axes, 0...  22.8 us
    all_to_all x2, waiting for transfers between devices, share(): lax.all_to_all(jnp.broadcast_to(vec[None], (count,) + vec.shape), axes, 0...  20.9 us
    all_to_all x1, waiting for transfers between devices, per_device(): lax.all_to_all(partial.reshape(nf, ny * rows // nf, cols), 'f', 0, 0, til...  19.7 us
    all_to_all x1, blocking collectives, share(): lax.all_to_all(jnp.broadcast_to(vec[None], (count,) + vec.shape), axes, 0...  16.8 us
    all_gather x2, waiting for transfers between devices, gather_rows(): whole = lax.all_gather(padded, axis, axis=0, tiled=False)  13.1 us
    all_to_all x1, starting transfers between devices, per_device(): lax.all_to_all(partial.reshape(nf, ny * rows // nf, cols), 'f', 0, 0, til...  9.13 us
  transfers between devices with their start and end apart: 9, of which 7 were waited for; matrix products, arithmetic and copies ran while one was open for 4% of the time, Pallas kernels for 0%

profile of v1, /device:TPU:1, one launch (start us, length us, event | category | flops | bytes accessed | tf_op | source)
XLA Modules:
  0.0 231.4 jit_solution(16084451471756805442)
XLA Ops:
  7.2 2.2 convert_reduce_fusion
  9.4 0.9 broadcast_in_dim.6
  10.3 17.1 %all-to-all-start = ((f32[64,1,1280]{2,1,0:T(1,128)}), f32[64,1,1280]{2,1,0:T(1,128)S(1)}, u32[]{:S(2)}, u32[]{:S(2)}) async-start(f32[64,1,1280]{2,1,0:T(1,128)} %broadcast_in_dim.6), calls=%async_computation | async-start | bytes 655360 | tf_op jit(solution)/shard_map/all_to_all | solution.py:15
  27.4 4.0 %collective-permute-start = (bf16[80,640]{1,0:T(8,128)(2,1)S(1)}, bf16[80,640]{1,0:T(8,128)(2,1)S(1)}, u32[]{:S(2)}, u32[]{:S(2)}) collective-permute-start(bf16[80,640]{1,0:T(8,128)(2,1)S(1)} %copy-done.2), channel_id=1, source_target_pairs={{0,0},{1,64},{2,128},{3,192},{4,256},{5,320},{6,384},{7,448},{64,1... | collective-permute-start | bytes 307208 | tf_op jit(solution)/shard_map/ppermute | solution.py:32
  31.5 9.7 %all-to-all-done = f32[64,1,1280]{2,1,0:T(1,128)S(1)} async-done(((f32[64,1,1280]{2,1,0:T(1,128)}), f32[64,1,1280]{2,1,0:T(1,128)S(1)}, u32[]{:S(2)}, u32[]{:S(2)}) %all-to-all-start) | async-done | bytes 327712 | tf_op jit(solution)/shard_map/all_to_all | solution.py:15
  41.2 0.2 reduce_sum.92
  41.5 0.7 pad.7
  42.2 0.7 all-gather.6.cloned.1.call-update
  42.9 0.1 multiply_reduce_fusion.1
  43.3 16.8 %all_to_all.39 = f32[8,1,1440]{2,1,0:T(1,128)S(1)} all-to-all(f32[8,1,1440]{2,1,0:T(1,128)S(1)} %broadcast_in_dim.7), channel_id=1, replica_groups=mesh['y'=8,'z'=8,'f'=8] {'f'}, dimensions={0} | all-to-all | bytes 92160 | tf_op jit(solution)/shard_map/all_to_all | solution.py:15
  60.1 0.7 broadcast_in_dim.8
  60.8 5.6 %all-to-all-start.2 = ((f32[64,1,160]{2,1,0:T(1,128)}), f32[64,1,160]{2,1,0:T(1,128)S(1)}, u32[]{:S(2)}, u32[]{:S(2)}) async-start(f32[64,1,160]{2,1,0:T(1,128)} %broadcast_in_dim.8), calls=%async_computation.2 | async-start | bytes 131072 | tf_op jit(solution)/shard_map/all_to_all | solution.py:15
  66.4 11.1 %all-to-all-done.2 = f32[64,1,160]{2,1,0:T(1,128)S(1)} async-done(((f32[64,1,160]{2,1,0:T(1,128)}), f32[64,1,160]{2,1,0:T(1,128)S(1)}, u32[]{:S(2)}, u32[]{:S(2)}) %all-to-all-start.2) | async-done | bytes 40992 | tf_op jit(solution)/shard_map/all_to_all | solution.py:15
  78.0 0.6 fusion
  80.2 0.9 all-gather.8.cloned.1.call-done
  81.2 1.2 slice.47
  82.4 41.7 %all-gather.6.cloned.1.call-done = f32[640,640]{1,0:T(8,128)} async-done(((f32[80,640]{1,0:T(8,128)}), f32[640,640]{1,0:T(8,128)}) %all-gather.6.cloned.1.call-update) | async-done | bytes 1638416 | tf_op jit(solution)/shard_map/all_gather | solution.py:30
  124.1 1.7 subtract_convert_fusion
  125.8 2.1 fusion.4
  127.8 9.1 %all-to-all-start.3 = ((f32[8,80,640]{2,1,0:T(8,128)}), f32[8,80,640]{2,1,0:T(8,128)S(1)}, u32[]{:S(2)}, u32[]{:S(2)}) async-start(f32[8,80,640]{2,1,0:T(8,128)} %fusion.4), calls=%async_computation.3 | async-start | bytes 3276800 | tf_op jit(solution)/shard_map/all_to_all | solution.py:63
  137.0 0.8 convert_bitcast_fusion
  137.8 0.7 pad.8
  138.5 19.7 %all-to-all-done.3 = f32[8,80,640]{2,1,0:T(8,128)S(1)} async-done(((f32[8,80,640]{2,1,0:T(8,128)}), f32[8,80,640]{2,1,0:T(8,128)S(1)}, u32[]{:S(2)}, u32[]{:S(2)}) %all-to-all-start.3) | async-done | bytes 1638432 | tf_op jit(solution)/shard_map/all_to_all | solution.py:63
  158.3 1.0 stack.2
  159.3 4.4 %all-to-all-start.4 = ((bf16[8,80,640]{2,1,0:T(8,128)(2,1)}), bf16[8,80,640]{2,1,0:T(8,128)(2,1)S(1)}, u32[]{:S(2)}, u32[]{:S(2)}) async-start(bf16[8,80,640]{2,1,0:T(8,128)(2,1)} %stack.2), calls=%async_computation.4 | async-start | bytes 1638400 | tf_op jit(solution)/shard_map/all_to_all | solution.py:67
  163.7 12.2 %all-gather.10.cloned.1.call-done = bf16[832,640]{1,0:T(8,128)(2,1)} async-done(((bf16[104,640]{1,0:T(8,128)(2,1)}), bf16[832,640]{1,0:T(8,128)(2,1)}) %all-gather.10.cloned.1.call-update) | async-done | bytes 1064976 | tf_op jit(solution)/shard_map/all_gather | solution.py:21
  175.9 1.2 slice.50
  177.1 2.1 fusion.5
  179.2 7.0 %all-to-all-start.5 = ((f32[8,80,640]{2,1,0:T(8,128)}), f32[8,80,640]{2,1,0:T(8,128)S(1)}, u32[]{:S(2)}, u32[]{:S(2)}) async-start(f32[8,80,640]{2,1,0:T(8,128)} %fusion.5), calls=%async_computation.5 | async-start | bytes 3276800 | tf_op jit(solution)/shard_map/all_to_all | solution.py:70
  186.3 0.8 multiply_subtract_fusion
  187.0 37.1 %all-to-all-done.5 = f32[8,80,640]{2,1,0:T(8,128)S(1)} async-done(((f32[8,80,640]{2,1,0:T(8,128)}), f32[8,80,640]{2,1,0:T(8,128)S(1)}, u32[]{:S(2)}, u32[]{:S(2)}) %all-to-all-start.5) | async-done | bytes 1638432 | tf_op jit(solution)/shard_map/all_to_all | solution.py:70
  224.1 0.7 reduce_sum.99
  (33 shorter events, 1.2 us)
Async XLA Ops:
  7.2 20.3 %copy-start.2 = (bf16[80,640]{1,0:T(8,128)(2,1)S(1)}, bf16[80,640]{1,0:T(8,128)(2,1)}, u32[]{:S(2)}) copy-start(bf16[80,640]{1,0:T(8,128)(2,1)} %param.7) | copy-start | bytes 307204
  7.2 35.8 %copy-start = (f32[80,640]{1,0:T(8,128)S(1)}, f32[80,640]{1,0:T(8,128)}, u32[]{:S(2)}) copy-start(f32[80,640]{1,0:T(8,128)} %param.8) | copy-start | bytes 614404
  9.4 33.7 %copy-start.1 = (f32[640,80]{0,1:T(8,128)S(1)}, f32[640,80]{0,1:T(8,128)}, u32[]{:S(2)}) copy-start(f32[640,80]{0,1:T(8,128)} %param.9) | copy-start | bytes 614404
  10.3 31.0 %all-to-all-start = ((f32[64,1,1280]{2,1,0:T(1,128)}), f32[64,1,1280]{2,1,0:T(1,128)S(1)}, u32[]{:S(2)}, u32[]{:S(2)}) async-start(f32[64,1,1280]{2,1,0:T(1,128)} %broadcast_in_dim.6), calls=%async_computation | async-start | bytes 655360 | tf_op jit(solution)/shard_map/all_to_all | solution.py:15
  27.4 53.8 %all-gather.8.cloned.1.call-start = ((), (), s32[]{:S(2)}) async-start(), calls=%async_computation.7 | async-start | bytes 1198080 | tf_op jit(solution)/shard_map/all_gather | solution.py:21
  27.4 14.0 %collective-permute-start = (bf16[80,640]{1,0:T(8,128)(2,1)S(1)}, bf16[80,640]{1,0:T(8,128)(2,1)S(1)}, u32[]{:S(2)}, u32[]{:S(2)}) collective-permute-start(bf16[80,640]{1,0:T(8,128)(2,1)S(1)} %copy-done.2), channel_id=1, source_target_pairs={{0,0},{1,64},{2,128},{3,192},{4,256},{5,320},{6,384},{7,448},{64,1... | collective-permute-start | bytes 307208 | tf_op jit(solution)/shard_map/ppermute | solution.py:32
  42.2 81.9 %all-gather.6.cloned.1.call-start = ((), (), s32[]{:S(2)}) async-start(), calls=%async_computation.6 | async-start | bytes 1843200 | tf_op jit(solution)/shard_map/all_gather | solution.py:30
  60.8 16.8 %all-to-all-start.2 = ((f32[64,1,160]{2,1,0:T(1,128)}), f32[64,1,160]{2,1,0:T(1,128)S(1)}, u32[]{:S(2)}, u32[]{:S(2)}) async-start(f32[64,1,160]{2,1,0:T(1,128)} %broadcast_in_dim.8), calls=%async_computation.2 | async-start | bytes 131072 | tf_op jit(solution)/shard_map/all_to_all | solution.py:15
  127.8 30.4 %all-to-all-start.3 = ((f32[8,80,640]{2,1,0:T(8,128)}), f32[8,80,640]{2,1,0:T(8,128)S(1)}, u32[]{:S(2)}, u32[]{:S(2)}) async-start(f32[8,80,640]{2,1,0:T(8,128)} %fusion.4), calls=%async_computation.3 | async-start | bytes 3276800 | tf_op jit(solution)/shard_map/all_to_all | solution.py:63
  137.0 38.9 %all-gather.10.cloned.1.call-start = ((), (), s32[]{:S(2)}) async-start(), calls=%async_computation.8 | async-start | bytes 1198080 | tf_op jit(solution)/shard_map/all_gather | solution.py:21
  159.3 17.8 %all-to-all-start.4 = ((bf16[8,80,640]{2,1,0:T(8,128)(2,1)}), bf16[8,80,640]{2,1,0:T(8,128)(2,1)S(1)}, u32[]{:S(2)}, u32[]{:S(2)}) async-start(bf16[8,80,640]{2,1,0:T(8,128)(2,1)} %stack.2), calls=%async_computation.4 | async-start | bytes 1638400 | tf_op jit(solution)/shard_map/all_to_all | solution.py:67
  179.2 44.9 %all-to-all-start.5 = ((f32[8,80,640]{2,1,0:T(8,128)}), f32[8,80,640]{2,1,0:T(8,128)S(1)}, u32[]{:S(2)}, u32[]{:S(2)}) async-start(f32[8,80,640]{2,1,0:T(8,128)} %fusion.5), calls=%async_computation.5 | async-start | bytes 3276800 | tf_op jit(solution)/shard_map/all_to_all | solution.py:70
Sparse Core Ops, SparseCore 0:
  42.3 38.8 all-gather.7
  83.2 40.7 all-gather.5
  140.4 35.4 all-gather.9
